TPU v7x, 32 devices: a whole 2x2x4 slice. The times are simulated.
32 devices in a mesh: dp: 4 (over y, core), ctx: 8 (over z, x).
Axes of the slice: x: 2, y: 2, z: 4, core: 2. Of those that a mesh axis runs over, the one named last changes fastest.
Arguments:
- queries: bfloat16 [4608, 256], P(('dp', 'ctx')), parts along dimension 0, may hold values from -5 to 5
- keys: bfloat16 [4608, 256], P(('dp', 'ctx')), parts along dimension 0, may hold values from -5 to 5
- values: bfloat16 [4608, 256], P(('dp', 'ctx')), parts along dimension 0, may hold values from -2.5 to 2.5
- out_grad: bfloat16 [4608, 256], P(('dp', 'ctx')), parts along dimension 0, may hold values from -5 to 5
- span_end: int32 [4608], P(('dp', 'ctx')), parts along dimension 0, may hold values from 0 to 1152, as said below
Outputs:
- output: bfloat16 [4608, 256], P(('dp', 'ctx')), parts along dimension 0
- query_grad: float32 [4608, 256], P(('dp', 'ctx')), parts along dimension 0
- key_grad: float32 [4608, 256], P(('dp', 'ctx')), parts along dimension 0
- value_grad: float32 [4608, 256], P(('dp', 'ctx')), parts along dimension 0
There are 4 independent parts, one for each index of `dp`. A program takes and returns all parts, laid end to end along the dimension named above; each array names one. Nothing has to cross between parts.
Inputs may be any that keep to these rules, and one draw needn't show every extreme that they name: `span_end`: image spans are runs of consecutive tokens, each of at most 288 tokens; every token of a span holds the position just past the span's last token; the last 288 tokens of a document form one span.
All inputs are finite; a program needn't handle non-finite values.
Results may differ from a plain program's by a relative error of at most 0.035.
Values may be sent and summed in bfloat16 or wider, within the bound.
A program may use at most 64 MiB of HBM per device.

v0:
```python
import jax
import jax.numpy as jnp
from jax import lax
from jax.sharding import PartitionSpec as P

HEADS = 2
HEAD_DIM = 128


def split_heads(matrix):
    return matrix.reshape(matrix.shape[0], HEADS, HEAD_DIM)


def local(queries, keys, values, out_grad, span_end):
    row_count = queries.shape[0]
    scaling = HEAD_DIM ** (-0.5)
    device = lax.axis_index("ctx")
    base_positions = device * row_count + jnp.arange(row_count, dtype=jnp.int32)
    base_limits = jnp.maximum(base_positions + 1, span_end)
    limit_all = lax.all_gather(base_limits, "ctx", axis=0, tiled=True)
    query_rows_own, key_rows_own, value_rows_own, grad_rows_own = (queries, keys, values, out_grad)
    query_own = split_heads(query_rows_own)
    key_own = split_heads(key_rows_own)
    value_own = split_heads(value_rows_own)
    grad_own = split_heads(grad_rows_own)

    def own_scores(key_piece):
        columns = jnp.arange(key_piece.shape[0], dtype=jnp.int32)
        visible = (columns[None, :] < base_limits[:, None])[None]
        scores = (
            jnp.einsum("qhd,khd->hqk", query_own, key_piece, preferred_element_type=jnp.float32)
            * scaling
        )
        return (scores, visible)

    pieces = (
        lax.all_gather(keys, "ctx", axis=0, tiled=True),
        lax.all_gather(values, "ctx", axis=0, tiled=True),
    )
    run_high = jnp.full((HEADS, row_count), -1e30, jnp.float32)
    weighted = jnp.zeros((row_count, HEADS, HEAD_DIM), jnp.float32)
    key_piece = split_heads(pieces[0])
    value_piece = split_heads(pieces[1])
    scores, visible = own_scores(key_piece)
    scores = jnp.where(visible, scores, -1e30)
    new_high = jnp.maximum(run_high, jnp.max(scores, axis=-1))
    factor = jnp.exp(run_high - new_high)
    weights_now = jnp.where(visible, jnp.exp(scores - new_high[..., None]), 0.0)
    run_total = jnp.sum(weights_now, axis=-1)
    weighted = weighted * factor.T[:, :, None] + jnp.einsum(
        "hqk,khd->qhd",
        weights_now,
        value_piece.astype(jnp.float32),
        precision=lax.Precision.HIGHEST,
        preferred_element_type=jnp.float32,
    )
    run_high, run_total, weighted = (new_high, run_total, weighted)
    log_total = run_high + jnp.log(run_total)
    output = (weighted / run_total.T[:, :, None]).astype(jnp.bfloat16)
    row_dot = jnp.sum(grad_own.astype(jnp.float32) * output.astype(jnp.float32), axis=-1).T
    pieces = (
        lax.all_gather(keys, "ctx", axis=0, tiled=True),
        lax.all_gather(values, "ctx", axis=0, tiled=True),
    )
    key_piece = split_heads(pieces[0])
    value_piece = split_heads(pieces[1])
    scores, visible = own_scores(key_piece)
    probs = jnp.where(visible, jnp.exp(scores - log_total[..., None]), 0.0)
    prob_grad = jnp.einsum(
        "qhd,khd->hqk", grad_own, value_piece, preferred_element_type=jnp.float32
    )
    score_grad = probs * (prob_grad - row_dot[..., None])
    query_grad = jnp.einsum(
        "hqk,khd->qhd",
        score_grad.astype(jnp.bfloat16),
        key_piece,
        preferred_element_type=jnp.float32,
    )
    log_all, dot_all = (
        lax.all_gather(log_total, "ctx", axis=1, tiled=True),
        lax.all_gather(row_dot, "ctx", axis=1, tiled=True),
    )
    pieces = (
        lax.all_gather(queries, "ctx", axis=0, tiled=True),
        lax.all_gather(out_grad, "ctx", axis=0, tiled=True),
    )
    query_piece = split_heads(pieces[0])
    grad_piece = split_heads(pieces[1])
    visible = (base_positions[None, :] < limit_all[:, None])[None]
    scores = (
        jnp.einsum("qhd,khd->hqk", query_piece, key_own, preferred_element_type=jnp.float32)
        * scaling
    )
    probs = jnp.where(visible, jnp.exp(scores - log_all[..., None]), 0.0)
    value_grad = jnp.einsum(
        "hqk,qhd->khd", probs.astype(jnp.bfloat16), grad_piece, preferred_element_type=jnp.float32
    )
    prob_grad = jnp.einsum(
        "qhd,khd->hqk", grad_piece, value_own, preferred_element_type=jnp.float32
    )
    score_grad = probs * (prob_grad - dot_all[..., None])
    key_grad = jnp.einsum(
        "hqk,qhd->khd",
        score_grad.astype(jnp.bfloat16),
        query_piece,
        preferred_element_type=jnp.float32,
    )
    key_grad, value_grad = (key_grad, value_grad)
    flat_shape = (row_count, HEADS * HEAD_DIM)
    results = (
        output.astype(jnp.float32).reshape(flat_shape),
        (query_grad * scaling).reshape(flat_shape),
        (key_grad * scaling).reshape(flat_shape),
        value_grad.reshape(flat_shape),
    )
    return (results[0].astype(jnp.bfloat16), results[1], results[2], results[3])


def solution(mesh):
    in_specs = (
        P(("dp", "ctx"), None),
        P(("dp", "ctx"), None),
        P(("dp", "ctx"), None),
        P(("dp", "ctx"), None),
        P(("dp", "ctx")),
    )
    out_specs = (
        P(("dp", "ctx"), None),
        P(("dp", "ctx"), None),
        P(("dp", "ctx"), None),
        P(("dp", "ctx"), None),
    )
    return jax.shard_map(local, mesh=mesh, in_specs=in_specs, out_specs=out_specs, check_vma=False)
```

profile of v0, /device:TPU:0, one launch (start us, length us, event | category | flops | bytes accessed | tf_op | source)
XLA Modules:
  0.0 201.7 jit_solution(14404172331278344812)
XLA Ops:
  0.6 0.0 copy-start
  0.6 1.3 dynamic-slice
  2.6 0.8 fusion.42
  3.4 0.2 iota_compare_fusion
  3.6 33.4 %all_gather.23 = bf16[1152,256]{1,0:T(8,128)(2,1)S(1)} all-gather(bf16[144,256]{1,0:T(8,128)(2,1)} %param.6), channel_id=1, replica_groups=mesh['dp'=4,'ctx'=8] {'ctx'}, dimensions={0}, use_global_device_ids=true | all-gather | bytes 663552 | tf_op jit(solution)/shard_map/all_gather | solution.py:37
  37.0 0.3 copy.28
  37.3 0.0 copy-done
  37.3 0.0 copy-start.1
  37.3 0.5 select_reduce_fusion
  37.8 0.0 copy-start.2
  37.8 0.5 fusion.16
  38.3 31.5 %all_gather.24 = bf16[1152,256]{1,0:T(8,128)(2,1)S(1)} all-gather(bf16[144,256]{1,0:T(8,128)(2,1)S(1)} %copy-done.1), channel_id=1, replica_groups=mesh['dp'=4,'ctx'=8] {'ctx'}, dimensions={0}, use_global_device_ids=true | all-gather | bytes 663552 | tf_op jit(solution)/shard_map/all_gather | solution.py:38
  69.8 0.3 copy.31
  70.1 1.2 multiply_reduce_fusion
  71.4 0.6 copy_bitcast_fusion.3
  72.0 0.7 fusion.10
  72.8 0.7 copy.92
  73.4 31.7 %all_gather.28 = bf16[1152,256]{1,0:T(8,128)(2,1)S(1)} all-gather(bf16[144,256]{1,0:T(8,128)(2,1)S(1)} %copy-done.2), channel_id=1, replica_groups=mesh['dp'=4,'ctx'=8] {'ctx'}, dimensions={0}, use_global_device_ids=true | all-gather | bytes 663552 | tf_op jit(solution)/shard_map/all_gather | solution.py:85
  105.1 0.3 copy.43
  105.4 0.0 copy-start.3
  105.4 31.4 %all_gather.26 = bf16[1152,256]{1,0:T(8,128)(2,1)S(1)} all-gather(bf16[144,256]{1,0:T(8,128)(2,1)S(1)} %copy-done), channel_id=1, replica_groups=mesh['dp'=4,'ctx'=8] {'ctx'}, dimensions={0}, use_global_device_ids=true | all-gather | bytes 663552 | tf_op jit(solution)/shard_map/all_gather | solution.py:84
  136.8 0.3 copy.39
  137.1 26.1 %all-gather = f32[8,144,2]{1,2,0:T(2,128)S(1)} all-gather(f32[1,144,2]{1,2,0:T(2,128)S(1)} %bitcast.105), channel_id=1, replica_groups=mesh['dp'=4,'ctx'=8] {'ctx'}, dimensions={0}, use_global_device_ids=true | all-gather | bytes 10368 | tf_op jit(solution)/shard_map/all_gather | solution.py:80
  163.2 0.1 reshape.122
  163.3 9.9 %all-reduce = s32[1152]{0:T(1024)S(1)} all-reduce(s32[1152]{0:T(1024)S(1)} %get-tuple-element.4), channel_id=1, replica_groups=mesh['dp'=4,'ctx'=8] {'ctx'}, use_global_device_ids=true, to_apply=%add | all-reduce | flops 1152 | bytes 9216
  173.2 0.2 broadcast_compare_fusion
  173.4 0.5 fusion.4
  173.9 0.3 convolution_bitcast_fusion
  174.3 26.1 %all-gather.1 = f32[8,144,2]{1,2,0:T(2,128)S(1)} all-gather(f32[1,144,2]{1,2,0:T(2,128)S(1)} %bitcast.107), channel_id=1, replica_groups=mesh['dp'=4,'ctx'=8] {'ctx'}, dimensions={0}, use_global_device_ids=true | all-gather | bytes 10368 | tf_op jit(solution)/shard_map/all_gather | solution.py:81
  200.4 0.1 reshape.124
  200.5 0.5 fusion.12
  201.0 0.7 copy_bitcast_fusion
  (9 shorter events, 0.0 us)
Async XLA Ops:
  0.6 36.7 %copy-start = (bf16[144,256]{1,0:T(8,128)(2,1)S(1)}, bf16[144,256]{1,0:T(8,128)(2,1)}, u32[]{:S(2)}) copy-start(bf16[144,256]{1,0:T(8,128)(2,1)} %param.5) | copy-start | bytes 221188
  37.3 1.0 copy-start.1
  37.8 32.3 %copy-start.2 = (bf16[144,256]{1,0:T(8,128)(2,1)S(1)}, bf16[144,256]{1,0:T(8,128)(2,1)}, u32[]{:S(2)}) copy-start(bf16[144,256]{1,0:T(8,128)(2,1)} %param.8) | copy-start | bytes 221188
  105.4 68.0 %copy-start.3 = (bf16[144,256]{1,0:T(8,128)(2,1)S(1)}, bf16[144,256]{1,0:T(8,128)(2,1)}, u32[]{:S(2)}) copy-start(bf16[144,256]{1,0:T(8,128)(2,1)} %param.6) | copy-start | bytes 221188
where the time goes:
time: 202 us
  blocking collectives  190 us (94%)
  local copies, waits for them, and re-layouts  4.71 us (2%)
  matrix products  3.81 us (2%)
    all_gather x1, blocking collectives, local(): lax.all_gather(keys, 'ctx', axis=0, tiled=True)  33.4 us
    all_gather x1, blocking collectives, local(): lax.all_gather(out_grad, 'ctx', axis=0, tiled=True)  31.7 us
    all_gather x1, blocking collectives, local(): lax.all_gather(values, 'ctx', axis=0, tiled=True)  31.5 us
    all_gather x1, blocking collectives, local(): lax.all_gather(queries, 'ctx', axis=0, tiled=True)  31.4 us
    all_gather x1, blocking collectives, local(): lax.all_gather(log_total, 'ctx', axis=1, tiled=True)  26.1 us
    all_gather x1, blocking collectives, local(): lax.all_gather(row_dot, 'ctx', axis=1, tiled=True)  26.1 us
    unnamed x1, blocking collectives  9.9 us

commit v1 on v0

v1 whole, which is shorter than its diff:
```python
import functools

import jax
import jax.numpy as jnp
from jax import lax
from jax.experimental import pallas as pl
from jax.experimental.pallas import tpu as pltpu
from jax.sharding import PartitionSpec as P

HEADS = 2
HEAD_DIM = 128
IMG = 288
HIDDEN = -1e30
KEY, VALUE, QUERY, GRAD = range(4)


def dot(a, b, a_dim, b_dim):
    return lax.dot_general(a, b, (((a_dim,), (b_dim,)), ((), ())), preferred_element_type=jnp.float32)


def kernel(
    n, rows,
    q_in, k_in, v_in, g_in, lim_ref,
    o_ref, dq_ref, dk_ref, dv_ref,
    buf, limits, st, dp, stats, top, acc_o, acc_q, acc_k, acc_v, res_out, res_in,
    send_sem, recv_sem, lim_send, lim_recv, stat_send, stat_recv, res_send, res_recv,
):
    scaling = HEAD_DIM ** -0.5
    blocks = n // HEADS
    span = HEADS * rows
    cut = blocks * span - IMG
    me = lax.axis_index("ctx")
    z = me // HEADS
    x = me % HEADS
    sources = (k_in, v_in, q_in, g_in)

    def device(index):
        return {"ctx": index}

    def needed(query_block, key_block):
        return (
            (key_block <= query_block)
            | ((query_block + 1) * span > cut)
            | ((key_block <= query_block + 1) & (key_block * span < cut))
        )

    ahead = (z + 1 < blocks) & needed(z, z + 1)
    behind = (z > 0) & needed(z - 1, z)

    barrier = pltpu.get_barrier_semaphore()
    for step in range(1, n):
        pl.semaphore_signal(barrier, inc=1, device_id=device(lax.rem(me + step, n)))
    pl.semaphore_wait(barrier, n - 1)

    own_rows = pl.ds(pl.multiple_of(x * rows, 16), rows)
    other_rows = pl.ds(pl.multiple_of((1 - x) * rows, 16), rows)

    def limit_copy(slot, target, send):
        return pltpu.make_async_remote_copy(
            src_ref=lim_ref, dst_ref=limits.at[slot], send_sem=lim_send.at[send],
            recv_sem=lim_recv.at[slot], device_id=device(target))

    def block_copy(array, target, head):
        return pltpu.make_async_remote_copy(
            src_ref=sources[array].at[:, pl.ds(head * HEAD_DIM, HEAD_DIM)],
            dst_ref=buf.at[array, z, own_rows],
            send_sem=send_sem.at[array, target, head],
            recv_sem=recv_sem.at[array, z, x],
            device_id=device(target * HEADS + head))

    def local_copy(array, target, head):
        return pltpu.make_async_copy(
            sources[array].at[:, pl.ds(head * HEAD_DIM, HEAD_DIM)],
            buf.at[array, z, own_rows],
            recv_sem.at[array, z, x])

    def stat_copy(target):
        return pltpu.make_async_remote_copy(
            src_ref=stats.at[z], dst_ref=stats.at[z], send_sem=stat_send.at[target],
            recv_sem=stat_recv.at[z], device_id=device(target * HEADS + x))

    def result_copy(slot):
        return pltpu.make_async_remote_copy(
            src_ref=res_out.at[slot], dst_ref=res_in.at[slot], send_sem=res_send.at[slot],
            recv_sem=res_recv.at[slot], device_id=device(z * HEADS + 1 - x))

    limit_copy(0, z * HEADS + 1 - x, 0).start()
    @pl.when(ahead)
    def _():
        for head in range(HEADS):
            limit_copy(1 + x, (z + 1) * HEADS + head, 1 + head).start()

    routes = []
    for step in range(blocks):
        for array, target in (
            (KEY, blocks - 1 - step), (VALUE, blocks - 1 - step), (QUERY, step), (GRAD, step)):
            wanted = needed(target, z) if array in (KEY, VALUE) else needed(z, target)
            for head in range(HEADS):
                routes.append((array, target, head, wanted))
    for array, target, head, wanted in routes:
        mine = target * HEADS + head == me
        @pl.when(wanted & mine)
        def _():
            local_copy(array, target, head).start()
        @pl.when(wanted & jnp.logical_not(mine))
        def _():
            block_copy(array, target, head).start()

    def arrive(array, block):
        for portion in range(HEADS):
            ref = buf.at[array, block, pl.ds(portion * rows, rows)]
            pltpu.make_async_copy(ref, ref, recv_sem.at[array, block, portion]).wait()

    for array in (KEY, QUERY, VALUE, GRAD):
        arrive(array, z)
    limit_copy(0, z * HEADS + 1 - x, 0).wait_recv()
    own_limit = jnp.maximum(lim_ref[...], limits[0])
    key_row = lax.broadcasted_iota(jnp.int32, (span, span), 0)
    top[...] = jnp.full_like(top, HIDDEN)

    def score(block, masked):
        if not (masked == "own"):
            arrive(KEY, block)
            arrive(VALUE, block)
        scores = dot(buf[KEY, block], buf[QUERY, z], 1, 1) * scaling
        if masked:
            scores = jnp.where(key_row + block * span < own_limit, scores, HIDDEN)
        st[block] = scores
        dp[block] = dot(buf[VALUE, block], buf[GRAD, z], 1, 1)
        top[...] = jnp.maximum(top[...], jnp.max(scores, axis=0, keepdims=True))

    score(z, "own")
    @pl.when(ahead)
    def _():
        score(z + 1, "ahead")

    @pl.loop(1, z + 1)
    def _(back):
        score(z - back, None)

    last = z + ahead.astype(jnp.int32) + 1
    highest = top[...]

    def total(block, carry):
        sums, dots = carry
        probs = jnp.exp(st[block] - highest)
        st[block] = probs
        return (sums + jnp.sum(probs, axis=0, keepdims=True),
                dots + jnp.sum(probs * dp[block], axis=0, keepdims=True))

    zero = jnp.zeros_like(highest)
    sums, dots = lax.fori_loop(0, last, total, (zero, zero))
    row_dot = dots / sums
    inverse = 1.0 / sums
    stats[z, 0:1] = highest + jnp.log(sums)
    stats[z, 1:2] = row_dot
    for target in range(blocks):
        @pl.when(needed(z, target) & (z != target))
        def _():
            stat_copy(target).start()

    def own_query(block):
        probs = st[block] * inverse
        score_grad = (probs * (dp[block] - row_dot)).astype(jnp.bfloat16)
        return probs.astype(jnp.bfloat16), score_grad

    probs, score_grad = own_query(z)
    acc_o[...] = dot(probs, buf[VALUE, z], 0, 0)
    acc_q[...] = dot(score_grad, buf[KEY, z], 0, 0)
    acc_v[...] = dot(probs, buf[GRAD, z], 1, 0)
    acc_k[...] = dot(score_grad, buf[QUERY, z], 1, 0)

    def add_query(block):
        probs, score_grad = own_query(block)
        acc_o[...] += dot(probs, buf[VALUE, block], 0, 0)
        acc_q[...] += dot(score_grad, buf[KEY, block], 0, 0)

    @pl.when(ahead)
    def _():
        add_query(z + 1)

    @pl.loop(1, z + 1)
    def _(back):
        add_query(z - back)

    res_out[0] = acc_o[other_rows, :].astype(jnp.bfloat16)
    result_copy(0).start()
    res_out[1] = (acc_q[other_rows, :] * scaling).astype(jnp.bfloat16)
    result_copy(1).start()

    def add_key(block, masked):
        arrive(QUERY, block)
        arrive(GRAD, block)
        scores = dot(buf[KEY, z], buf[QUERY, block], 1, 1) * scaling
        if masked:
            limit_copy(1, 0, 1).wait_recv()
            limit_copy(2, 0, 1).wait_recv()
            limit = jnp.maximum(limits[1], limits[2])
            scores = jnp.where(key_row + z * span < limit, scores, HIDDEN)
        prob_grad = dot(buf[VALUE, z], buf[GRAD, block], 1, 1)
        pltpu.make_async_copy(stats.at[block], stats.at[block], stat_recv.at[block]).wait()
        probs = jnp.exp(scores - stats[block, 0:1])
        score_grad = (probs * (prob_grad - stats[block, 1:2])).astype(jnp.bfloat16)
        acc_v[...] += dot(probs.astype(jnp.bfloat16), buf[GRAD, block], 1, 0)
        acc_k[...] += dot(score_grad, buf[QUERY, block], 1, 0)

    @pl.when(behind)
    def _():
        add_key(z - 1, True)

    @pl.loop(z + 1, blocks)
    def _(block):
        add_key(block, False)

    res_out[2] = (acc_k[other_rows, :] * scaling).astype(jnp.bfloat16)
    result_copy(2).start()
    res_out[3] = acc_v[other_rows, :].astype(jnp.bfloat16)
    result_copy(3).start()

    own_columns = pl.ds(pl.multiple_of(x * HEAD_DIM, HEAD_DIM), HEAD_DIM)
    other_columns = pl.ds(pl.multiple_of((1 - x) * HEAD_DIM, HEAD_DIM), HEAD_DIM)
    o_ref[:, own_columns] = acc_o[own_rows, :].astype(jnp.bfloat16)
    dq_ref[:, own_columns] = acc_q[own_rows, :] * scaling
    dk_ref[:, own_columns] = acc_k[own_rows, :] * scaling
    dv_ref[:, own_columns] = acc_v[own_rows, :]
    for slot, ref in enumerate((o_ref, dq_ref, dk_ref, dv_ref)):
        result_copy(slot).wait_recv()
        ref[:, other_columns] = res_in[slot].astype(ref.dtype)

    for slot in range(4):
        result_copy(slot).wait_send()
    limit_copy(0, 0, 0).wait_send()
    @pl.when(ahead)
    def _():
        for head in range(HEADS):
            limit_copy(0, 0, 1 + head).wait_send()
    for target in range(blocks):
        @pl.when(needed(z, target) & (z != target))
        def _():
            stat_copy(target).wait_send()
    for array, target, head, wanted in routes:
        @pl.when(wanted & (target * HEADS + head != me))
        def _():
            block_copy(array, target, head).wait_send()


def solution(mesh):
    n = mesh.shape["ctx"]

    def local(queries, keys, values, out_grad, span_end):
        rows = queries.shape[0]
        blocks, span = n // HEADS, HEADS * rows
        device = lax.axis_index("ctx")
        offset = lax.rem(device, HEADS) * rows
        positions = device * rows + jnp.arange(rows, dtype=jnp.int32)
        limit = jnp.maximum(positions + 1, span_end)
        limit = lax.dynamic_update_slice(jnp.zeros((1, span), jnp.int32), limit[None], (0, offset))
        f32, bf16 = jnp.float32, jnp.bfloat16
        anywhere = pl.BlockSpec(memory_space=pl.ANY)
        vmem = pl.BlockSpec(memory_space=pltpu.VMEM)
        dma = pltpu.SemaphoreType.DMA
        return pl.pallas_call(
            functools.partial(kernel, n, rows),
            out_shape=tuple(
                jax.ShapeDtypeStruct(queries.shape, kind) for kind in (bf16, f32, f32, f32)),
            in_specs=[anywhere] * 4 + [vmem],
            out_specs=(vmem,) * 4,
            scratch_shapes=[
                pltpu.VMEM((4, blocks, span, HEAD_DIM), bf16),
                pltpu.VMEM((3, 1, span), jnp.int32),
                pltpu.VMEM((blocks, span, span), f32),
                pltpu.VMEM((blocks, span, span), f32),
                pltpu.VMEM((blocks, 2, span), f32),
                pltpu.VMEM((1, span), f32),
                pltpu.VMEM((span, HEAD_DIM), f32),
                pltpu.VMEM((span, HEAD_DIM), f32),
                pltpu.VMEM((span, HEAD_DIM), f32),
                pltpu.VMEM((span, HEAD_DIM), f32),
                pltpu.VMEM((4, rows, HEAD_DIM), bf16),
                pltpu.VMEM((4, rows, HEAD_DIM), bf16),
                dma((4, blocks, HEADS)),
                dma((4, blocks, HEADS)),
                dma((3,)),
                dma((3,)),
                dma((blocks,)),
                dma((blocks,)),
                dma((4,)),
                dma((4,)),
            ],
            compiler_params=pltpu.CompilerParams(collective_id=0, has_side_effects=True),
        )(queries, keys, values, out_grad, limit)

    spec = P(("dp", "ctx"), None)
    return jax.shard_map(
        local, mesh=mesh, in_specs=(spec,) * 4 + (P(("dp", "ctx")),),
        out_specs=(spec,) * 4, check_vma=False)
```

time: 202 us -> 40.4 us (0.20)
  blocking collectives: 190 us -> 0 us
  Pallas kernels: 0 us -> 33.9 us
  matrix products: 3.81 us -> 0 us
    all_gather x6 -> x0, blocking collectives: 180 us -> none  [the longest x1 33.4 us: local(): lax.all_gather(keys, 'ctx', axis=0, tiled=True)]
    pallas_call x0 -> x1, Pallas kernels: none -> 33.9 us  [local(): pl.pallas_call(functools.partial(kernel, n, rows), out_shape=tuple((jax.S...]
    unnamed x1 -> x0, blocking collectives: 9.9 us -> none
    unnamed x12 -> x14, local copies, waits for them, and re-layouts: 1.48 us -> 5.38 us
    dot_general x6 -> x0, matrix products: 3.81 us -> none  [the longest x1 1.23 us: local(): jnp.einsum('hqk,khd->qhd', weights_now, value_piece.astype(jnp.float32),...]
where the time goes in v1:
time: 40.4 us; the launch traced here: 40.1 us
  Pallas kernels  33.9 us (84%)
  local copies, waits for them, and re-layouts  5.52 us (14%)
  between operations  0.69 us (2%)
    pallas_call x1, Pallas kernels, local(): pl.pallas_call(functools.partial(kernel, n, rows), out_shape=tuple((jax.S...  33.9 us
    unnamed x14, local copies, waits for them, and re-layouts  5.38 us

profile of v1, /device:TPU:0, one launch (start us, length us, event | category | flops | bytes accessed | tf_op | source)
XLA Modules:
  0.0 40.1 jit_solution(6825812031824218168)
XLA Ops:
  0.6 0.0 copy-start.4
  0.7 0.7 %copy-done.4 = s32[144]{0:T(256)S(1)} copy-done((s32[144]{0:T(256)S(1)}, s32[144]{0:T(256)}, u32[]{:S(2)}) %copy-start.4) | copy-done | bytes 600
  1.3 0.1 dynamic_update_slice.3.lim_ref
  1.5 0.0 copy-start.3
  1.5 0.6 %copy-done.3 = s32[1,288]{1,0:T(1,128)} copy-done((s32[1,288]{1,0:T(1,128)}, s32[1,288]{1,0:T(1,128)S(1)}, u32[]{:S(2)}) %copy-start.3) | copy-done | bytes 1176
  2.0 33.9 %shard_map.84 = (bf16[144,256]{1,0:T(8,128)(2,1)}, f32[144,256]{1,0:T(8,128)}, f32[144,256]{1,0:T(8,128)}, f32[144,256]{1,0:T(8,128)}) custom-call(bf16[144,256]{1,0:T(8,128)(2,1)} %q_in.1, bf16[144,256]{1,0:T(8,128)(2,1)} %k_in.1, bf16[144,256]{1,0:T(8,128)(2,1)} %v_in.1, bf16[144,256]{1,0:T(8,128)(2,1)} %g_in.1, s32[1,288]{1,0:T(1,128)} %copy-done.3), custom_call_target="tpu_custom_call" | custom-call | tf_op jit(solution)/shard_map/pallas_call | solution.py:262
  35.9 0.0 copy-start.2
  35.9 1.6 %copy.14 = bf16[144,256]{1,0:T(8,128)(2,1)} copy(bf16[144,256]{1,0:T(8,128)(2,1)} %get-tuple-element.8) | data formatting | bytes 147456
  37.5 0.0 copy-done.2
  37.5 0.0 copy-start.1
  37.5 0.7 %copy.15 = f32[144,256]{1,0:T(8,128)} copy(f32[144,256]{1,0:T(8,128)S(1)} %copy-done.2) | data formatting | bytes 294912
  38.2 0.3 copy-done.1
  38.5 0.0 copy-start
  38.5 0.7 %copy.16 = f32[144,256]{1,0:T(8,128)} copy(f32[144,256]{1,0:T(8,128)S(1)} %copy-done.1) | data formatting | bytes 294912
  39.1 0.3 copy-done
  39.4 0.7 %copy.17 = f32[144,256]{1,0:T(8,128)} copy(f32[144,256]{1,0:T(8,128)S(1)} %copy-done) | data formatting | bytes 294912
  (2 shorter events, 0.0 us)
Async XLA Ops:
  0.6 0.7 %copy-start.4 = (s32[144]{0:T(256)S(1)}, s32[144]{0:T(256)}, u32[]{:S(2)}) copy-start(s32[144]{0:T(256)} %param.9) | copy-start | bytes 1732
  1.5 0.6 %copy-start.3 = (s32[1,288]{1,0:T(1,128)}, s32[1,288]{1,0:T(1,128)S(1)}, u32[]{:S(2)}) copy-start(s32[1,288]{1,0:T(1,128)S(1)} %dynamic_update_slice.3.lim_ref) | copy-start | bytes 3460
  35.9 1.6 %copy-start.2 = (f32[144,256]{1,0:T(8,128)S(1)}, f32[144,256]{1,0:T(8,128)}, u32[]{:S(2)}) copy-start(f32[144,256]{1,0:T(8,128)} %get-tuple-element.9) | copy-start | bytes 442372
  37.5 1.0 %copy-start.1 = (f32[144,256]{1,0:T(8,128)S(1)}, f32[144,256]{1,0:T(8,128)}, u32[]{:S(2)}) copy-start(f32[144,256]{1,0:T(8,128)} %get-tuple-element.10) | copy-start | bytes 442372
  38.5 1.0 %copy-start = (f32[144,256]{1,0:T(8,128)S(1)}, f32[144,256]{1,0:T(8,128)}, u32[]{:S(2)}) copy-start(f32[144,256]{1,0:T(8,128)} %get-tuple-element.11) | copy-start | bytes 442372

commit v2 on v1

--- a/solution.py
+++ b/solution.py
@@ -10,6 +10,7 @@
 HEADS = 2
 HEAD_DIM = 128
 IMG = 288
+DIRECT = 2
 HIDDEN = -1e30
 KEY, VALUE, QUERY, GRAD = range(4)
 
@@ -20,10 +21,10 @@
 
 def kernel(
     n, rows,
-    q_in, k_in, v_in, g_in, lim_ref,
+    q_in, k_in, v_in, g_in, ends_in,
     o_ref, dq_ref, dk_ref, dv_ref,
-    buf, limits, st, dp, stats, top, acc_o, acc_q, acc_k, acc_v, res_out, res_in,
-    send_sem, recv_sem, lim_send, lim_recv, stat_send, stat_recv, res_send, res_recv,
+    buf, ends, st, dp, st_key, dp_key, stats, top, acc_o, acc_q, acc_k, acc_v, res_out, res_in,
+    send_sem, recv_sem, lim_send, lim_recv, stat_send, stat_recv, res_send, res_recv, pass_send, pass_recv,
 ):
     scaling = HEAD_DIM ** -0.5
     blocks = n // HEADS
@@ -50,15 +51,27 @@
     barrier = pltpu.get_barrier_semaphore()
     for step in range(1, n):
         pl.semaphore_signal(barrier, inc=1, device_id=device(lax.rem(me + step, n)))
-    pl.semaphore_wait(barrier, n - 1)
-
     own_rows = pl.ds(pl.multiple_of(x * rows, 16), rows)
     other_rows = pl.ds(pl.multiple_of((1 - x) * rows, 16), rows)
 
+    own_columns = pl.ds(pl.multiple_of(x * HEAD_DIM, HEAD_DIM), HEAD_DIM)
+    other_columns = pl.ds(pl.multiple_of((1 - x) * HEAD_DIM, HEAD_DIM), HEAD_DIM)
+
     def limit_copy(slot, target, send):
         return pltpu.make_async_remote_copy(
-            src_ref=lim_ref, dst_ref=limits.at[slot], send_sem=lim_send.at[send],
+            src_ref=ends_in, dst_ref=ends.at[slot], send_sem=lim_send.at[send],
             recv_sem=lim_recv.at[slot], device_id=device(target))
+
+    def own_limit_copy():
+        return pltpu.make_async_copy(ends_in, ends.at[x], lim_recv.at[x])
+
+    def limits(block, slot):
+        for portion in range(HEADS):
+            ref = ends.at[slot + portion]
+            pltpu.make_async_copy(ref, ref, lim_recv.at[slot + portion]).wait()
+        joined = jnp.concatenate([ends[slot + portion] for portion in range(HEADS)], axis=1)
+        position = lax.broadcasted_iota(jnp.int32, (1, span), 1) + block * span
+        return jnp.maximum(position + 1, joined)
 
     def block_copy(array, target, head):
         return pltpu.make_async_remote_copy(
@@ -68,9 +81,9 @@
             recv_sem=recv_sem.at[array, z, x],
             device_id=device(target * HEADS + head))
 
-    def local_copy(array, target, head):
+    def local_copy(array):
         return pltpu.make_async_copy(
-            sources[array].at[:, pl.ds(head * HEAD_DIM, HEAD_DIM)],
+            sources[array].at[:, own_columns],
             buf.at[array, z, own_rows],
             recv_sem.at[array, z, x])
 
@@ -84,44 +97,73 @@
             src_ref=res_out.at[slot], dst_ref=res_in.at[slot], send_sem=res_send.at[slot],
             recv_sem=res_recv.at[slot], device_id=device(z * HEADS + 1 - x))
 
-    limit_copy(0, z * HEADS + 1 - x, 0).start()
+    own_limit_copy().start()
+    for array in range(4):
+        local_copy(array).start()
+    pl.semaphore_wait(barrier, n - 1)
+
+    limit_copy(x, z * HEADS + 1 - x, 0).start()
     @pl.when(ahead)
     def _():
         for head in range(HEADS):
-            limit_copy(1 + x, (z + 1) * HEADS + head, 1 + head).start()
+            limit_copy(HEADS + x, (z + 1) * HEADS + head, 1 + head).start()
 
     routes = []
     for step in range(blocks):
         for array, target in (
             (KEY, blocks - 1 - step), (VALUE, blocks - 1 - step), (QUERY, step), (GRAD, step)):
             wanted = needed(target, z) if array in (KEY, VALUE) else needed(z, target)
+            near = (target - z <= DIRECT) & (z - target <= DIRECT)
             for head in range(HEADS):
-                routes.append((array, target, head, wanted))
+                away = target * HEADS + head != me
+                routes.append((array, target, head, wanted & near & away))
     for array, target, head, wanted in routes:
-        mine = target * HEADS + head == me
-        @pl.when(wanted & mine)
-        def _():
-            local_copy(array, target, head).start()
-        @pl.when(wanted & jnp.logical_not(mine))
+        @pl.when(wanted)
         def _():
             block_copy(array, target, head).start()
 
-    def arrive(array, block):
+    def forward_copy(array, block):
+        target = z + 1 if array in (KEY, VALUE) else z - 1
+        return pltpu.make_async_remote_copy(
+            src_ref=buf.at[array, block], dst_ref=buf.at[array, block],
+            send_sem=pass_send.at[array, block], recv_sem=pass_recv.at[array, block],
+            device_id=device(target * HEADS + x))
+
+    def forwards(array, block):
+        if array in (KEY, VALUE):
+            return (z - block >= DIRECT) & (z + 1 < blocks)
+        return (block - z >= DIRECT) & (z > 0)
+
+    def arrive_direct(array, block):
         for portion in range(HEADS):
             ref = buf.at[array, block, pl.ds(portion * rows, rows)]
             pltpu.make_async_copy(ref, ref, recv_sem.at[array, block, portion]).wait()
 
+    def arrive(arrays, block):
+        near = (block - z <= DIRECT) & (z - block <= DIRECT)
+        @pl.when(near)
+        def _():
+            for array in arrays:
+                arrive_direct(array, block)
+        @pl.when(jnp.logical_not(near))
+        def _():
+            for array in arrays:
+                ref = buf.at[array, block]
+                pltpu.make_async_copy(ref, ref, pass_recv.at[array, block]).wait()
+        @pl.when(forwards(arrays[0], block))
+        def _():
+            for array in arrays:
+                forward_copy(array, block).start()
+
     for array in (KEY, QUERY, VALUE, GRAD):
-        arrive(array, z)
-    limit_copy(0, z * HEADS + 1 - x, 0).wait_recv()
-    own_limit = jnp.maximum(lim_ref[...], limits[0])
+        arrive_direct(array, z)
+    own_limit = limits(z, 0)
     key_row = lax.broadcasted_iota(jnp.int32, (span, span), 0)
     top[...] = jnp.full_like(top, HIDDEN)
 
     def score(block, masked):
         if not (masked == "own"):
-            arrive(KEY, block)
-            arrive(VALUE, block)
+            arrive((KEY, VALUE), block)
         scores = dot(buf[KEY, block], buf[QUERY, z], 1, 1) * scaling
         if masked:
             scores = jnp.where(key_row + block * span < own_limit, scores, HIDDEN)
@@ -159,6 +201,26 @@
         def _():
             stat_copy(target).start()
 
+    def key_score(block, masked):
+        if masked:
+            for array in (QUERY, GRAD):
+                arrive_direct(array, block)
+        else:
+            arrive((QUERY, GRAD), block)
+        scores = dot(buf[KEY, z], buf[QUERY, block], 1, 1) * scaling
+        if masked:
+            scores = jnp.where(key_row + z * span < limits(block, HEADS), scores, HIDDEN)
+        st_key[block] = scores
+        dp_key[block] = dot(buf[VALUE, z], buf[GRAD, block], 1, 1)
+
+    @pl.when(behind)
+    def _():
+        key_score(z - 1, True)
+
+    @pl.loop(z + 1, blocks)
+    def _(block):
+        key_score(block, False)
+
     def own_query(block):
         probs = st[block] * inverse
         score_grad = (probs * (dp[block] - row_dot)).astype(jnp.bfloat16)
@@ -188,37 +250,26 @@
     res_out[1] = (acc_q[other_rows, :] * scaling).astype(jnp.bfloat16)
     result_copy(1).start()
 
-    def add_key(block, masked):
-        arrive(QUERY, block)
-        arrive(GRAD, block)
-        scores = dot(buf[KEY, z], buf[QUERY, block], 1, 1) * scaling
-        if masked:
-            limit_copy(1, 0, 1).wait_recv()
-            limit_copy(2, 0, 1).wait_recv()
-            limit = jnp.maximum(limits[1], limits[2])
-            scores = jnp.where(key_row + z * span < limit, scores, HIDDEN)
-        prob_grad = dot(buf[VALUE, z], buf[GRAD, block], 1, 1)
+    def add_key(block):
         pltpu.make_async_copy(stats.at[block], stats.at[block], stat_recv.at[block]).wait()
-        probs = jnp.exp(scores - stats[block, 0:1])
-        score_grad = (probs * (prob_grad - stats[block, 1:2])).astype(jnp.bfloat16)
+        probs = jnp.exp(st_key[block] - stats[block, 0:1])
+        score_grad = (probs * (dp_key[block] - stats[block, 1:2])).astype(jnp.bfloat16)
         acc_v[...] += dot(probs.astype(jnp.bfloat16), buf[GRAD, block], 1, 0)
         acc_k[...] += dot(score_grad, buf[QUERY, block], 1, 0)
 
     @pl.when(behind)
     def _():
-        add_key(z - 1, True)
+        add_key(z - 1)
 
     @pl.loop(z + 1, blocks)
     def _(block):
-        add_key(block, False)
+        add_key(block)
 
     res_out[2] = (acc_k[other_rows, :] * scaling).astype(jnp.bfloat16)
     result_copy(2).start()
     res_out[3] = acc_v[other_rows, :].astype(jnp.bfloat16)
     result_copy(3).start()
 
-    own_columns = pl.ds(pl.multiple_of(x * HEAD_DIM, HEAD_DIM), HEAD_DIM)
-    other_columns = pl.ds(pl.multiple_of((1 - x) * HEAD_DIM, HEAD_DIM), HEAD_DIM)
     o_ref[:, own_columns] = acc_o[own_rows, :].astype(jnp.bfloat16)
     dq_ref[:, own_columns] = acc_q[own_rows, :] * scaling
     dk_ref[:, own_columns] = acc_k[own_rows, :] * scaling
@@ -239,9 +290,15 @@
         def _():
             stat_copy(target).wait_send()
     for array, target, head, wanted in routes:
-        @pl.when(wanted & (target * HEADS + head != me))
+        @pl.when(wanted)
         def _():
             block_copy(array, target, head).wait_send()
+    for arrays in ((KEY, VALUE), (QUERY, GRAD)):
+        for block in range(blocks):
+            @pl.when(forwards(arrays[0], block))
+            def _():
+                for array in arrays:
+                    forward_copy(array, block).wait_send()
 
 
 def solution(mesh):
@@ -250,11 +307,6 @@
     def local(queries, keys, values, out_grad, span_end):
         rows = queries.shape[0]
         blocks, span = n // HEADS, HEADS * rows
-        device = lax.axis_index("ctx")
-        offset = lax.rem(device, HEADS) * rows
-        positions = device * rows + jnp.arange(rows, dtype=jnp.int32)
-        limit = jnp.maximum(positions + 1, span_end)
-        limit = lax.dynamic_update_slice(jnp.zeros((1, span), jnp.int32), limit[None], (0, offset))
         f32, bf16 = jnp.float32, jnp.bfloat16
         anywhere = pl.BlockSpec(memory_space=pl.ANY)
         vmem = pl.BlockSpec(memory_space=pltpu.VMEM)
@@ -263,11 +315,13 @@
             functools.partial(kernel, n, rows),
             out_shape=tuple(
                 jax.ShapeDtypeStruct(queries.shape, kind) for kind in (bf16, f32, f32, f32)),
-            in_specs=[anywhere] * 4 + [vmem],
+            in_specs=[anywhere] * 5,
             out_specs=(vmem,) * 4,
             scratch_shapes=[
                 pltpu.VMEM((4, blocks, span, HEAD_DIM), bf16),
-                pltpu.VMEM((3, 1, span), jnp.int32),
+                pltpu.VMEM((2 * HEADS, 1, rows), jnp.int32),
+                pltpu.VMEM((blocks, span, span), f32),
+                pltpu.VMEM((blocks, span, span), f32),
                 pltpu.VMEM((blocks, span, span), f32),
                 pltpu.VMEM((blocks, span, span), f32),
                 pltpu.VMEM((blocks, 2, span), f32),
@@ -281,14 +335,16 @@
                 dma((4, blocks, HEADS)),
                 dma((4, blocks, HEADS)),
                 dma((3,)),
-                dma((3,)),
+                dma((2 * HEADS,)),
                 dma((blocks,)),
                 dma((blocks,)),
                 dma((4,)),
                 dma((4,)),
+                dma((4, blocks)),
+                dma((4, blocks)),
             ],
             compiler_params=pltpu.CompilerParams(collective_id=0, has_side_effects=True),
-        )(queries, keys, values, out_grad, limit)
+        )(queries, keys, values, out_grad, span_end[None])
 
     spec = P(("dp", "ctx"), None)
     return jax.shard_map(

time: 40.4 us -> 39.2 us (0.970)
  local copies, waits for them, and re-layouts: 5.52 us -> 4.15 us
    unnamed x14 -> x10, local copies, waits for them, and re-layouts: 5.38 us -> 4.15 us
where the time goes in v2:
time: 39.2 us; the launch traced here: 39 us
  Pallas kernels  34.2 us (87%)
  local copies, waits for them, and re-layouts  4.15 us (11%)
  between operations  0.65 us (2%)
    pallas_call x1, Pallas kernels, local(): pl.pallas_call(functools.partial(kernel, n, rows), out_shape=tuple((jax.S...  34.2 us
    unnamed x10, local copies, waits for them, and re-layouts  4.15 us

profile of v2, /device:TPU:0, one launch (start us, length us, event | category | flops | bytes accessed | tf_op | source)
XLA Modules:
  0.0 39.0 jit_solution(848785093897762227)
XLA Ops:
  0.6 34.2 %shard_map.84 = (bf16[144,256]{1,0:T(8,128)(2,1)}, f32[144,256]{1,0:T(8,128)}, f32[144,256]{1,0:T(8,128)}, f32[144,256]{1,0:T(8,128)}) custom-call(bf16[144,256]{1,0:T(8,128)(2,1)} %q_in.1, bf16[144,256]{1,0:T(8,128)(2,1)} %k_in.1, bf16[144,256]{1,0:T(8,128)(2,1)} %v_in.1, bf16[144,256]{1,0:T(8,128)(2,1)} %g_in.1, s32[1,144]{1,0:T(1,128)} %bitcast.1), custom_call_target="tpu_custom_call" | custom-call | tf_op jit(solution)/shard_map/pallas_call | solution.py:314
  34.8 0.0 copy-start.2
  34.8 1.6 %copy.13 = bf16[144,256]{1,0:T(8,128)(2,1)} copy(bf16[144,256]{1,0:T(8,128)(2,1)} %get-tuple-element.8) | data formatting | bytes 147456
  36.4 0.0 copy-done.2
  36.4 0.0 copy-start.1
  36.4 0.7 %copy.14 = f32[144,256]{1,0:T(8,128)} copy(f32[144,256]{1,0:T(8,128)S(1)} %copy-done.2) | data formatting | bytes 294912
  37.1 0.3 copy-done.1
  37.4 0.0 copy-start
  37.4 0.7 %copy.15 = f32[144,256]{1,0:T(8,128)} copy(f32[144,256]{1,0:T(8,128)S(1)} %copy-done.1) | data formatting | bytes 294912
  38.0 0.3 copy-done
  38.3 0.7 %copy.16 = f32[144,256]{1,0:T(8,128)} copy(f32[144,256]{1,0:T(8,128)S(1)} %copy-done) | data formatting | bytes 294912
Async XLA Ops:
  34.8 1.6 %copy-start.2 = (f32[144,256]{1,0:T(8,128)S(1)}, f32[144,256]{1,0:T(8,128)}, u32[]{:S(2)}) copy-start(f32[144,256]{1,0:T(8,128)} %get-tuple-element.9) | copy-start | bytes 442372
  36.4 1.0 %copy-start.1 = (f32[144,256]{1,0:T(8,128)S(1)}, f32[144,256]{1,0:T(8,128)}, u32[]{:S(2)}) copy-start(f32[144,256]{1,0:T(8,128)} %get-tuple-element.10) | copy-start | bytes 442372
  37.4 1.0 %copy-start = (f32[144,256]{1,0:T(8,128)S(1)}, f32[144,256]{1,0:T(8,128)}, u32[]{:S(2)}) copy-start(f32[144,256]{1,0:T(8,128)} %get-tuple-element.11) | copy-start | bytes 442372

commit v3 on v2

--- a/solution.py
+++ b/solution.py
@@ -49,8 +49,17 @@
     behind = (z > 0) & needed(z - 1, z)
 
     barrier = pltpu.get_barrier_semaphore()
-    for step in range(1, n):
-        pl.semaphore_signal(barrier, inc=1, device_id=device(lax.rem(me + step, n)))
+    def close(target):
+        return (target - z <= DIRECT) & (z - target <= DIRECT)
+
+    met = -1
+    for target in range(blocks):
+        met = met + HEADS * close(target).astype(jnp.int32)
+        for head in range(HEADS):
+            @pl.when(close(target) & (target * HEADS + head != me))
+            def _():
+                pl.semaphore_signal(barrier, inc=1, device_id=device(target * HEADS + head))
+
     own_rows = pl.ds(pl.multiple_of(x * rows, 16), rows)
     other_rows = pl.ds(pl.multiple_of((1 - x) * rows, 16), rows)
 
@@ -100,7 +109,7 @@
     own_limit_copy().start()
     for array in range(4):
         local_copy(array).start()
-    pl.semaphore_wait(barrier, n - 1)
+    pl.semaphore_wait(barrier, met)
 
     limit_copy(x, z * HEADS + 1 - x, 0).start()
     @pl.when(ahead)
@@ -113,7 +122,7 @@
         for array, target in (
             (KEY, blocks - 1 - step), (VALUE, blocks - 1 - step), (QUERY, step), (GRAD, step)):
             wanted = needed(target, z) if array in (KEY, VALUE) else needed(z, target)
-            near = (target - z <= DIRECT) & (z - target <= DIRECT)
+            near = close(target)
             for head in range(HEADS):
                 away = target * HEADS + head != me
                 routes.append((array, target, head, wanted & near & away))
@@ -139,21 +148,32 @@
             ref = buf.at[array, block, pl.ds(portion * rows, rows)]
             pltpu.make_async_copy(ref, ref, recv_sem.at[array, block, portion]).wait()
 
+    def arrive_forwarded(array, block):
+        ref = buf.at[array, block]
+        pltpu.make_async_copy(ref, ref, pass_recv.at[array, block]).wait()
+
+    def relay(arrays, block):
+        @pl.when(forwards(arrays[0], block))
+        def _():
+            for array in arrays:
+                @pl.when(close(block))
+                def _():
+                    arrive_direct(array, block)
+                @pl.when(jnp.logical_not(close(block)))
+                def _():
+                    arrive_forwarded(array, block)
+                forward_copy(array, block).start()
+
     def arrive(arrays, block):
-        near = (block - z <= DIRECT) & (z - block <= DIRECT)
-        @pl.when(near)
+        held = forwards(arrays[0], block)
+        @pl.when(close(block) & jnp.logical_not(held))
         def _():
             for array in arrays:
                 arrive_direct(array, block)
-        @pl.when(jnp.logical_not(near))
+        @pl.when(jnp.logical_not(close(block) | held))
         def _():
             for array in arrays:
-                ref = buf.at[array, block]
-                pltpu.make_async_copy(ref, ref, pass_recv.at[array, block]).wait()
-        @pl.when(forwards(arrays[0], block))
-        def _():
-            for array in arrays:
-                forward_copy(array, block).start()
+                arrive_forwarded(array, block)
 
     for array in (KEY, QUERY, VALUE, GRAD):
         arrive_direct(array, z)
@@ -172,6 +192,12 @@
         top[...] = jnp.maximum(top[...], jnp.max(scores, axis=0, keepdims=True))
 
     score(z, "own")
+
+    @pl.loop(0, blocks)
+    def _(block):
+        relay((KEY, VALUE), block)
+        relay((QUERY, GRAD), block)
+
     @pl.when(ahead)
     def _():
         score(z + 1, "ahead")
@@ -200,6 +226,35 @@
         @pl.when(needed(z, target) & (z != target))
         def _():
             stat_copy(target).start()
+
+    def own_query(block):
+        probs = st[block] * inverse
+        score_grad = (probs * (dp[block] - row_dot)).astype(jnp.bfloat16)
+        return probs.astype(jnp.bfloat16), score_grad
+
+    probs, score_grad = own_query(z)
+    acc_o[...] = dot(probs, buf[VALUE, z], 0, 0)
+    acc_q[...] = dot(score_grad, buf[KEY, z], 0, 0)
+    acc_v[...] = dot(probs, buf[GRAD, z], 1, 0)
+    acc_k[...] = dot(score_grad, buf[QUERY, z], 1, 0)
+
+    def add_query(block):
+        probs, score_grad = own_query(block)
+        acc_o[...] += dot(probs, buf[VALUE, block], 0, 0)
+        acc_q[...] += dot(score_grad, buf[KEY, block], 0, 0)
+
+    @pl.when(ahead)
+    def _():
+        add_query(z + 1)
+
+    @pl.loop(1, z + 1)
+    def _(back):
+        add_query(z - back)
+
+    res_out[0] = acc_o[other_rows, :].astype(jnp.bfloat16)
+    result_copy(0).start()
+    res_out[1] = (acc_q[other_rows, :] * scaling).astype(jnp.bfloat16)
+    result_copy(1).start()
 
     def key_score(block, masked):
         if masked:
@@ -221,60 +276,37 @@
     def _(block):
         key_score(block, False)
 
-    def own_query(block):
-        probs = st[block] * inverse
-        score_grad = (probs * (dp[block] - row_dot)).astype(jnp.bfloat16)
-        return probs.astype(jnp.bfloat16), score_grad
-
-    probs, score_grad = own_query(z)
-    acc_o[...] = dot(probs, buf[VALUE, z], 0, 0)
-    acc_q[...] = dot(score_grad, buf[KEY, z], 0, 0)
-    acc_v[...] = dot(probs, buf[GRAD, z], 1, 0)
-    acc_k[...] = dot(score_grad, buf[QUERY, z], 1, 0)
-
-    def add_query(block):
-        probs, score_grad = own_query(block)
-        acc_o[...] += dot(probs, buf[VALUE, block], 0, 0)
-        acc_q[...] += dot(score_grad, buf[KEY, block], 0, 0)
-
-    @pl.when(ahead)
-    def _():
-        add_query(z + 1)
-
-    @pl.loop(1, z + 1)
-    def _(back):
-        add_query(z - back)
-
-    res_out[0] = acc_o[other_rows, :].astype(jnp.bfloat16)
-    result_copy(0).start()
-    res_out[1] = (acc_q[other_rows, :] * scaling).astype(jnp.bfloat16)
-    result_copy(1).start()
-
-    def add_key(block):
+    def add_value(block):
         pltpu.make_async_copy(stats.at[block], stats.at[block], stat_recv.at[block]).wait()
         probs = jnp.exp(st_key[block] - stats[block, 0:1])
-        score_grad = (probs * (dp_key[block] - stats[block, 1:2])).astype(jnp.bfloat16)
         acc_v[...] += dot(probs.astype(jnp.bfloat16), buf[GRAD, block], 1, 0)
+        st_key[block] = probs
+
+    def add_key(block):
+        score_grad = (st_key[block] * (dp_key[block] - stats[block, 1:2])).astype(jnp.bfloat16)
         acc_k[...] += dot(score_grad, buf[QUERY, block], 1, 0)
 
-    @pl.when(behind)
-    def _():
-        add_key(z - 1)
-
-    @pl.loop(z + 1, blocks)
-    def _(block):
-        add_key(block)
-
-    res_out[2] = (acc_k[other_rows, :] * scaling).astype(jnp.bfloat16)
-    result_copy(2).start()
-    res_out[3] = acc_v[other_rows, :].astype(jnp.bfloat16)
-    result_copy(3).start()
+    for step in (add_value, add_key):
+        @pl.when(behind)
+        def _():
+            step(z - 1)
+
+        @pl.loop(z + 1, blocks)
+        def _(block):
+            step(block)
+
+        if step is add_value:
+            res_out[3] = acc_v[other_rows, :].astype(jnp.bfloat16)
+            result_copy(3).start()
+        else:
+            res_out[2] = (acc_k[other_rows, :] * scaling).astype(jnp.bfloat16)
+            result_copy(2).start()
 
     o_ref[:, own_columns] = acc_o[own_rows, :].astype(jnp.bfloat16)
     dq_ref[:, own_columns] = acc_q[own_rows, :] * scaling
     dk_ref[:, own_columns] = acc_k[own_rows, :] * scaling
     dv_ref[:, own_columns] = acc_v[own_rows, :]
-    for slot, ref in enumerate((o_ref, dq_ref, dk_ref, dv_ref)):
+    for slot, ref in ((0, o_ref), (1, dq_ref), (3, dv_ref), (2, dk_ref)):
         result_copy(slot).wait_recv()
         ref[:, other_columns] = res_in[slot].astype(ref.dtype)
 
@@ -301,6 +333,15 @@
                     forward_copy(array, block).wait_send()
 
 
+def flush(*refs):
+    sem = refs[-1]
+    copies = [pltpu.make_async_copy(refs[i], refs[i + 4], sem.at[i]) for i in range(4)]
+    for copy in copies:
+        copy.start()
+    for copy in copies:
+        copy.wait()
+
+
 def solution(mesh):
     n = mesh.shape["ctx"]
 
@@ -311,10 +352,10 @@
         anywhere = pl.BlockSpec(memory_space=pl.ANY)
         vmem = pl.BlockSpec(memory_space=pltpu.VMEM)
         dma = pltpu.SemaphoreType.DMA
-        return pl.pallas_call(
+        results = pl.pallas_call(
             functools.partial(kernel, n, rows),
             out_shape=tuple(
-                jax.ShapeDtypeStruct(queries.shape, kind) for kind in (bf16, f32, f32, f32)),
+                pltpu.VMEM(queries.shape, kind) for kind in (bf16, f32, f32, f32)),
             in_specs=[anywhere] * 5,
             out_specs=(vmem,) * 4,
             scratch_shapes=[
@@ -345,6 +386,14 @@
             ],
             compiler_params=pltpu.CompilerParams(collective_id=0, has_side_effects=True),
         )(queries, keys, values, out_grad, span_end[None])
+        return pl.pallas_call(
+            flush,
+            out_shape=tuple(
+                jax.ShapeDtypeStruct(queries.shape, kind) for kind in (bf16, f32, f32, f32)),
+            in_specs=[vmem] * 4,
+            out_specs=(anywhere,) * 4,
+            scratch_shapes=[dma((4,))],
+        )(*(pltpu.with_memory_space_constraint(result, pltpu.VMEM) for result in results))
 
     spec = P(("dp", "ctx"), None)
     return jax.shard_map(

time: 39.2 us -> 30.7 us (0.78)
  Pallas kernels: 34.2 us -> 29.9 us
  local copies, waits for them, and re-layouts: 4.15 us -> 0 us
    pallas_call x1 -> x2, Pallas kernels: 34.2 us -> 29.9 us  [the longest x1 29.1 us: local(): pl.pallas_call(functools.partial(kernel, n, rows), out_shape=tuple((pltpu...]
    unnamed x10 -> x0, local copies, waits for them, and re-layouts: 4.15 us -> none
where the time goes in v3:
time: 30.7 us; the launch traced here: 30.6 us
  Pallas kernels  29.9 us (97%)
  between operations  0.64 us (2%)
    pallas_call x1, Pallas kernels, local(): pl.pallas_call(functools.partial(kernel, n, rows), out_shape=tuple((pltpu...  29.1 us
    pallas_call x1, Pallas kernels, local(): pl.pallas_call(flush, out_shape=tuple((jax.ShapeDtypeStruct(queries.shape...  0.82 us

profile of v3, /device:TPU:0, one launch (start us, length us, event | category | flops | bytes accessed | tf_op | source)
XLA Modules:
  0.0 30.6 jit_solution(6396582440921217359)
XLA Ops:
  0.6 29.1 %shard_map.84 = (bf16[144,256]{1,0:T(8,128)(2,1)S(1)}, f32[144,256]{1,0:T(8,128)S(1)}, f32[144,256]{1,0:T(8,128)S(1)}, f32[144,256]{1,0:T(8,128)S(1)}) custom-call(bf16[144,256]{1,0:T(8,128)(2,1)} %q_in.1, bf16[144,256]{1,0:T(8,128)(2,1)} %k_in.1, bf16[144,256]{1,0:T(8,128)(2,1)} %v_in.1, bf16[144,256]{1,0:T(8,128)(2,1)} %g_in.1, s32[1,144]{1,0:T(1,128)} %bitcast.1), custom_call_target="tpu_custom_call" | custom-call | tf_op jit(solution)/shard_map/pallas_call | solution.py:355
  29.8 0.8 %shard_map.85 = (bf16[144,256]{1,0:T(8,128)(2,1)}, f32[144,256]{1,0:T(8,128)}, f32[144,256]{1,0:T(8,128)}, f32[144,256]{1,0:T(8,128)}) custom-call(bf16[144,256]{1,0:T(8,128)(2,1)S(1)} %get-tuple-element.8.refs_0_, f32[144,256]{1,0:T(8,128)S(1)} %get-tuple-element.9.refs_1_, f32[144,256]{1,0:T(8,128)S(1)} %get-tuple-element.10.refs_2_, ...), custom_call_target="tpu_custom_call" | custom-call | tf_op jit(solution)/shard_map/pallas_call | solution.py:389

commit v4 on v3

--- a/solution.py
+++ b/solution.py
@@ -118,14 +118,14 @@
             limit_copy(HEADS + x, (z + 1) * HEADS + head, 1 + head).start()
 
     routes = []
-    for step in range(blocks):
-        for array, target in (
-            (KEY, blocks - 1 - step), (VALUE, blocks - 1 - step), (QUERY, step), (GRAD, step)):
-            wanted = needed(target, z) if array in (KEY, VALUE) else needed(z, target)
-            near = close(target)
-            for head in range(HEADS):
-                away = target * HEADS + head != me
-                routes.append((array, target, head, wanted & near & away))
+    order = [(array, blocks - 1 - step) for step in range(blocks) for array in (KEY, VALUE)]
+    order += [(array, step) for step in range(blocks) for array in (QUERY, GRAD)]
+    for array, target in order:
+        wanted = needed(target, z) if array in (KEY, VALUE) else needed(z, target)
+        near = close(target)
+        for head in range(HEADS):
+            away = target * HEADS + head != me
+            routes.append((array, target, head, wanted & near & away))
     for array, target, head, wanted in routes:
         @pl.when(wanted)
         def _():
@@ -175,11 +175,17 @@
             for array in arrays:
                 arrive_forwarded(array, block)
 
+    @pl.loop(0, blocks)
+    def _(block):
+        relay((KEY, VALUE), block)
+        relay((QUERY, GRAD), block)
+
     for array in (KEY, QUERY, VALUE, GRAD):
         arrive_direct(array, z)
     own_limit = limits(z, 0)
     key_row = lax.broadcasted_iota(jnp.int32, (span, span), 0)
-    top[...] = jnp.full_like(top, HIDDEN)
+    top[0:1] = jnp.full((1, span), HIDDEN, jnp.float32)
+    top[1:3] = jnp.zeros((2, span), jnp.float32)
 
     def score(block, masked):
         if not (masked == "own"):
@@ -188,15 +194,16 @@
         if masked:
             scores = jnp.where(key_row + block * span < own_limit, scores, HIDDEN)
         st[block] = scores
-        dp[block] = dot(buf[VALUE, block], buf[GRAD, z], 1, 1)
-        top[...] = jnp.maximum(top[...], jnp.max(scores, axis=0, keepdims=True))
+        prob_grad = dot(buf[VALUE, block], buf[GRAD, z], 1, 1)
+        dp[block] = prob_grad
+        highest = jnp.maximum(top[0:1], jnp.max(scores, axis=0, keepdims=True))
+        probs = jnp.exp(scores - highest)
+        factor = jnp.exp(top[0:1] - highest)
+        top[0:1] = highest
+        top[1:2] = top[1:2] * factor + jnp.sum(probs, axis=0, keepdims=True)
+        top[2:3] = top[2:3] * factor + jnp.sum(probs * prob_grad, axis=0, keepdims=True)
 
     score(z, "own")
-
-    @pl.loop(0, blocks)
-    def _(block):
-        relay((KEY, VALUE), block)
-        relay((QUERY, GRAD), block)
 
     @pl.when(ahead)
     def _():
@@ -206,21 +213,9 @@
     def _(back):
         score(z - back, None)
 
-    last = z + ahead.astype(jnp.int32) + 1
-    highest = top[...]
-
-    def total(block, carry):
-        sums, dots = carry
-        probs = jnp.exp(st[block] - highest)
-        st[block] = probs
-        return (sums + jnp.sum(probs, axis=0, keepdims=True),
-                dots + jnp.sum(probs * dp[block], axis=0, keepdims=True))
-
-    zero = jnp.zeros_like(highest)
-    sums, dots = lax.fori_loop(0, last, total, (zero, zero))
-    row_dot = dots / sums
-    inverse = 1.0 / sums
-    stats[z, 0:1] = highest + jnp.log(sums)
+    log_total = top[0:1] + jnp.log(top[1:2])
+    row_dot = top[2:3] / top[1:2]
+    stats[z, 0:1] = log_total
     stats[z, 1:2] = row_dot
     for target in range(blocks):
         @pl.when(needed(z, target) & (z != target))
@@ -228,7 +223,7 @@
             stat_copy(target).start()
 
     def own_query(block):
-        probs = st[block] * inverse
+        probs = jnp.exp(st[block] - log_total)
         score_grad = (probs * (dp[block] - row_dot)).astype(jnp.bfloat16)
         return probs.astype(jnp.bfloat16), score_grad
 
@@ -276,31 +271,38 @@
     def _(block):
         key_score(block, False)
 
-    def add_value(block):
+    def arrive_stats(block):
         pltpu.make_async_copy(stats.at[block], stats.at[block], stat_recv.at[block]).wait()
-        probs = jnp.exp(st_key[block] - stats[block, 0:1])
-        acc_v[...] += dot(probs.astype(jnp.bfloat16), buf[GRAD, block], 1, 0)
-        st_key[block] = probs
-
-    def add_key(block):
-        score_grad = (st_key[block] * (dp_key[block] - stats[block, 1:2])).astype(jnp.bfloat16)
-        acc_k[...] += dot(score_grad, buf[QUERY, block], 1, 0)
-
-    for step in (add_value, add_key):
-        @pl.when(behind)
-        def _():
-            step(z - 1)
-
-        @pl.loop(z + 1, blocks)
-        def _(block):
-            step(block)
-
-        if step is add_value:
-            res_out[3] = acc_v[other_rows, :].astype(jnp.bfloat16)
-            result_copy(3).start()
-        else:
-            res_out[2] = (acc_k[other_rows, :] * scaling).astype(jnp.bfloat16)
-            result_copy(2).start()
+
+    def add_key(block, part):
+        probs = jnp.exp(st_key[block, part] - stats[block, 0:1])
+        acc_v[part] += dot(probs.astype(jnp.bfloat16), buf[GRAD, block], 1, 0)
+        score_grad = (probs * (dp_key[block, part] - stats[block, 1:2])).astype(jnp.bfloat16)
+        acc_k[part] += dot(score_grad, buf[QUERY, block], 1, 0)
+
+    @pl.when(behind)
+    def _():
+        arrive_stats(z - 1)
+        add_key(z - 1, slice(None))
+
+    @pl.loop(z + 1, blocks - 1)
+    def _(block):
+        arrive_stats(block)
+        add_key(block, slice(None))
+
+    @pl.when(z < blocks - 1)
+    def _():
+        arrive_stats(blocks - 1)
+        add_key(blocks - 1, other_rows)
+
+    res_out[3] = acc_v[other_rows, :].astype(jnp.bfloat16)
+    result_copy(3).start()
+    res_out[2] = (acc_k[other_rows, :] * scaling).astype(jnp.bfloat16)
+    result_copy(2).start()
+
+    @pl.when(z < blocks - 1)
+    def _():
+        add_key(blocks - 1, own_rows)
 
     o_ref[:, own_columns] = acc_o[own_rows, :].astype(jnp.bfloat16)
     dq_ref[:, own_columns] = acc_q[own_rows, :] * scaling
@@ -366,7 +368,7 @@
                 pltpu.VMEM((blocks, span, span), f32),
                 pltpu.VMEM((blocks, span, span), f32),
                 pltpu.VMEM((blocks, 2, span), f32),
-                pltpu.VMEM((1, span), f32),
+                pltpu.VMEM((3, span), f32),
                 pltpu.VMEM((span, HEAD_DIM), f32),
                 pltpu.VMEM((span, HEAD_DIM), f32),
                 pltpu.VMEM((span, HEAD_DIM), f32),

time: 30.7 us -> 27.8 us (0.906)
  Pallas kernels: 29.9 us -> 27 us
    pallas_call x1, Pallas kernels: 29.1 us -> 26.2 us  [local(): pl.pallas_call(functools.partial(kernel, n, rows), out_shape=tuple((pltpu...]
where the time goes in v4:
time: 27.8 us; the launch traced here: 27.6 us
  Pallas kernels  27 us (97%)
  between operations  0.64 us (2%)
    pallas_call x1, Pallas kernels, local(): pl.pallas_call(functools.partial(kernel, n, rows), out_shape=tuple((pltpu...  26.2 us
    pallas_call x1, Pallas kernels, local(): pl.pallas_call(flush, out_shape=tuple((jax.ShapeDtypeStruct(queries.shape...  0.82 us

profile of v4, /device:TPU:0, one launch (start us, length us, event | category | flops | bytes accessed | tf_op | source)
XLA Modules:
  0.0 27.6 jit_solution(16591606311169168646)
XLA Ops:
  0.6 26.2 %shard_map.84 = (bf16[144,256]{1,0:T(8,128)(2,1)S(1)}, f32[144,256]{1,0:T(8,128)S(1)}, f32[144,256]{1,0:T(8,128)S(1)}, f32[144,256]{1,0:T(8,128)S(1)}) custom-call(bf16[144,256]{1,0:T(8,128)(2,1)} %q_in.1, bf16[144,256]{1,0:T(8,128)(2,1)} %k_in.1, bf16[144,256]{1,0:T(8,128)(2,1)} %v_in.1, bf16[144,256]{1,0:T(8,128)(2,1)} %g_in.1, s32[1,144]{1,0:T(1,128)} %bitcast.1), custom_call_target="tpu_custom_call" | custom-call | tf_op jit(solution)/shard_map/pallas_call | solution.py:357
  26.8 0.8 %shard_map.85 = (bf16[144,256]{1,0:T(8,128)(2,1)}, f32[144,256]{1,0:T(8,128)}, f32[144,256]{1,0:T(8,128)}, f32[144,256]{1,0:T(8,128)}) custom-call(bf16[144,256]{1,0:T(8,128)(2,1)S(1)} %get-tuple-element.8.refs_0_, f32[144,256]{1,0:T(8,128)S(1)} %get-tuple-element.9.refs_1_, f32[144,256]{1,0:T(8,128)S(1)} %get-tuple-element.10.refs_2_, ...), custom_call_target="tpu_custom_call" | custom-call | tf_op jit(solution)/shard_map/pallas_call | solution.py:391
